TPU v7x, 32 devices: a whole 2x2x4 slice. The times are simulated.
32 devices in a mesh: pp: 4 (over y, x), cp: 4 (over z), tp: 2 (over core).
Axes of the slice: x: 2, y: 2, z: 4, core: 2. Of those that a mesh axis runs over, the one named last changes fastest.
Arguments:
- queries: bfloat16 [2048, 16384], P(('pp', 'cp'), 'tp'), may hold values from -12 to 12
- keys: bfloat16 [2048, 1024], P(('pp', 'cp'), 'tp'), may hold values from -12 to 12
- values: bfloat16 [2048, 1024], P(('pp', 'cp'), 'tp'), may hold values from -6 to 6
- pair_order: int32 [4, 4], replicated, may hold values from 0 to 3, each once within a row
- lengths: int32 [4, 2], replicated, may hold values from 128 to 256
- routes: int32 [4, 512, 1], P(None, 'cp'), may hold values from 0 to 7; in each aligned block of 128 rows (0 to 127, 128 to 255, ..., all dimensions but the last counted through in order) at most 32 rows name the same one
Outputs:
- rebalanced: bfloat16 [4096, 16384], P(('pp', 'cp', 'tp'))
Inputs may be any that keep to these rules, and one draw needn't show every extreme that they name: `routes`: at most 32 rows of one device's block name the same destination, and in some block one destination is named by exactly 32 rows.
All inputs are finite; a program needn't handle non-finite values.
Results may differ from a plain program's by a relative error of at most 0.003.
Values may be sent and summed in bfloat16 or wider, within the bound.
No kernel may reach another device: no remote copies, remote signals or barrier semaphores. Data moves between devices by JAX's collectives and lax.ppermute only.
A program may use at most 64 MiB of HBM per device.

v0:
```python
import jax
import jax.numpy as jnp
from jax import lax
from jax.sharding import PartitionSpec as P

HD = 128
masked_score = -1e30


def shifted(block, axis, distance):
    devices = range(lax.axis_size(axis))
    route = [((i - distance) % len(devices), i) for i in devices]
    return lax.ppermute(block, axis, route)


def pair_positions(pair_ids, block_len, cycle_size):
    offsets = jnp.arange(block_len, dtype=jnp.int32)
    first_half = pair_ids[:, None] * block_len + offsets[None, :]
    second_half = (2 * cycle_size - 1 - pair_ids)[:, None] * block_len + offsets[None, :]
    return jnp.concatenate([first_half, second_half], axis=1)


def dispatch_rows(attended, targets, dest_count, capacity):
    row_count = attended.shape[0]
    matches = targets[:, None] == jnp.arange(dest_count, dtype=jnp.int32)[None, :]
    row_ids = jnp.arange(row_count, dtype=jnp.int32)
    earlier = (row_ids[None, :] < row_ids[:, None]).astype(jnp.bfloat16)
    before = jnp.dot(earlier, matches.astype(jnp.bfloat16), preferred_element_type=jnp.float32)
    slot_index = jnp.sum(jnp.where(matches, before, 0.0), axis=1).astype(jnp.int32)
    slot_ids = jnp.arange(capacity, dtype=jnp.int32)
    picked_rows = jnp.logical_and(
        jnp.transpose(matches)[:, None, :], slot_index[None, None, :] == slot_ids[None, :, None]
    )
    selector = picked_rows.astype(jnp.bfloat16).reshape(dest_count * capacity, row_count)
    return jnp.dot(selector, attended, preferred_element_type=jnp.float32).astype(jnp.bfloat16)


def spread_rows(buffer, cycle_size, split_size, capacity, width):
    flat_buffer = buffer.reshape(cycle_size * split_size, capacity, width)
    moved = lax.all_to_all(flat_buffer, ("cp", "tp"), split_axis=0, concat_axis=0, tiled=True)
    moved = jnp.transpose(moved.reshape(cycle_size, split_size, capacity, width), (0, 2, 1, 3))
    return moved.reshape(cycle_size * capacity, split_size * width)


def arrange_rows(attended, routes, source, cycle_size, split_size):
    row_count, width = attended.shape
    dest_count = cycle_size * split_size
    capacity = 2 * row_count // dest_count
    targets = lax.dynamic_index_in_dim(routes, source, 0, keepdims=False)[:, 0]
    buffer = dispatch_rows(attended, targets, dest_count, capacity)
    buffer = buffer.reshape(cycle_size, split_size, capacity, width)
    return spread_rows(buffer, cycle_size, split_size, capacity, width)


def body(queries, keys, values, pair_order, lengths, routes):
    cycle_size = lax.axis_size("cp")
    split_size = lax.axis_size("tp")
    section = lax.axis_index("pp")
    place = lax.axis_index("cp")
    row_count = queries.shape[0]
    block_len = row_count // 4
    width = queries.shape[1]
    group_count = keys.shape[1] // HD
    group_size = width // keys.shape[1]
    score_scale = HD ** (-0.5)
    order_row = lax.dynamic_index_in_dim(pair_order, section, 0, keepdims=False)
    own_pair = lax.dynamic_index_in_dim(order_row, place, 0, keepdims=True)
    query_pos = pair_positions(own_pair, block_len, cycle_size).reshape(2 * block_len)
    limits = lax.dynamic_index_in_dim(lengths, section, 0, keepdims=False)
    query_rows = queries.reshape(2, 2 * block_len, group_count, group_size, HD)
    stat_shape = (2, 2 * block_len, group_count, group_size)
    start_state = (
        jnp.full(stat_shape, masked_score, jnp.float32),
        jnp.zeros(stat_shape, jnp.float32),
        jnp.zeros(stat_shape + (HD,), jnp.float32),
    )
    state = start_state
    key_piece = lax.all_gather(keys, "cp", axis=0, tiled=True)
    value_piece = lax.all_gather(values, "cp", axis=0, tiled=True)
    shard_count = key_piece.shape[0] // row_count
    first_shard = jnp.int32(0) // row_count
    for base in range(0, shard_count, 4):
        block = min(4, shard_count - base)
        key_block = key_piece[base * row_count : (base + block) * row_count].reshape(
            block, 2, 2 * block_len, group_count, HD
        )
        value_block = value_piece[base * row_count : (base + block) * row_count].reshape(
            block, 2, 2 * block_len, group_count, HD
        )
        shard_ids = first_shard + base + jnp.arange(block, dtype=jnp.int32)
        key_pos = pair_positions(order_row[shard_ids], block_len, cycle_size).reshape(
            block * 2 * block_len
        )
        allowed = jnp.logical_and(
            key_pos[None, None, :] <= query_pos[None, :, None],
            key_pos[None, None, :] < limits[:, None, None],
        )
        allowed = allowed[:, :, None, None, :]
        scores = jnp.einsum(
            "sqgrd,nskgd->sqgrnk", query_rows, key_block, preferred_element_type=jnp.float32
        )
        scores = scores.reshape(stat_shape + (block * 2 * block_len,)) * score_scale
        running_max, running_total, running_sum = state
        block_max = jnp.max(jnp.where(allowed, scores, masked_score), axis=4)
        new_max = jnp.maximum(running_max, block_max)
        weights = jnp.where(allowed, jnp.exp(scores - new_max[..., None]), 0.0)
        carry_factor = jnp.exp(running_max - new_max)
        running_total = running_total * carry_factor + jnp.sum(weights, axis=4)
        shaped = weights.astype(jnp.bfloat16).reshape(stat_shape + (block, 2 * block_len))
        running_sum = running_sum * carry_factor[..., None] + jnp.einsum(
            "sqgrnk,nskgd->sqgrd", shaped, value_block, preferred_element_type=jnp.float32
        )
        state = (new_max, running_total, running_sum)
    attended = (state[2] / state[1][..., None]).astype(jnp.bfloat16).reshape(row_count, width)
    arranged = arrange_rows(attended, routes, section, cycle_size, split_size)
    return shifted(arranged, "pp", 1)


def solution(mesh):
    placed = (
        P(("pp", "cp"), "tp"),
        P(("pp", "cp"), "tp"),
        P(("pp", "cp"), "tp"),
        P(),
        P(),
        P(None, "cp", None),
    )
    return jax.shard_map(
        body, mesh=mesh, in_specs=placed, out_specs=P(("pp", "cp", "tp"), None), check_vma=False
    )
```

profile of v0, /device:TPU:0, one launch (start us, length us, event | category | flops | bytes accessed | tf_op | source)
XLA Modules:
  0.0 287.3 jit_solution(959507155664328261)
XLA Ops:
  0.0 0.7 copy-done
  0.7 0.1 fusion.9
  0.9 0.7 fusion.14
  1.6 1.3 dynamic_slice.18
  4.1 0.6 gather_fusion
  4.8 0.9 dynamic-slice_reduce_fusion
  6.1 2.2 copy.30
  8.3 17.4 %all_gather.6 = bf16[512,512]{1,0:T(8,128)(2,1)S(1)} all-gather(bf16[128,512]{1,0:T(8,128)(2,1)S(1)} %copy-done.2), channel_id=1, replica_groups=mesh['pp'=4,'cp'=4,'tp'=2] {'cp'}, dimensions={0}, use_global_device_ids=true | all-gather | bytes 655360 | tf_op jit(solution)/shard_map/all_gather | solution.py:78
  25.8 0.1 broadcast_and_fusion
  25.9 5.5 %fusion = (f32[2,64,4,16]{1,3,2,0:T(8,128)S(1)}, f32[2,4,4,64,64,16]{4,3,5,2,1,0:T(8,128)S(1)}) fusion(pred[2,64,4,64]{1,3,2,0:T(8,128)(4,1)S(1)} %broadcast_and_fusion, bf16[2,64,4,16,128,1]{4,3,2,1,0,5:T(8,128)(2,1)S(1)} %bitcast.52, bf16[4,2,64,4,128,1]{4,3,2,1,0,5:T(4,128)(2,1)S(1)} %bitcast.54), kind=kOutput, calls=%fused_computation.3 | convolution fusion | flops 543154176 | bytes 11075584 | tf_op jit(solution)/shard_map/sqgrd,nskgd->sqgrnk/dot_general | solution.py:99
  31.4 6.2 %fusion.3 = (f32[2,64,4,16]{1,3,2,0:T(8,128)S(1)}, bf16[2,64,4,16,4,64]{1,5,3,4,2,0:T(8,128)(2,1)}) fusion(f32[2,4,4,64,64,16]{4,3,5,2,1,0:T(8,128)S(1)} %get-tuple-element.12, f32[2,64,4,16]{1,3,2,0:T(8,128)S(1)} %broadcast_maximum_fusion, pred[2,64,4,64]{1,3,2,0:T(8,128)(4,1)S(1)} %broadcast_and_fusion), kind=kLoop, calls=%fused_computation.6 | loop fusion | flops 10477568 | bytes 12681216 | tf_op jit(solution)/shard_map/reduce_sum | solution.py:108
  37.8 0.1 copy.17
  38.0 17.2 %copy.15 = bf16[2,64,4,16,4,64]{5,3,4,1,2,0:T(8,128)(2,1)} copy(bf16[2,64,4,16,4,64]{1,5,3,4,2,0:T(8,128)(2,1)} %get-tuple-element.6) | data formatting | bytes 8388608 | tf_op jit(solution)/shard_map/convert_element_type | solution.py:109
  55.2 16.2 %all_gather.7 = bf16[512,512]{1,0:T(8,128)(2,1)S(1)} all-gather(bf16[128,512]{1,0:T(8,128)(2,1)S(1)} %copy-done.3), channel_id=1, replica_groups=mesh['pp'=4,'cp'=4,'tp'=2] {'cp'}, dimensions={0}, use_global_device_ids=true | all-gather | bytes 655360 | tf_op jit(solution)/shard_map/all_gather | solution.py:79
  71.6 5.7 %fusion.6 = bf16[2,64,4,16,128]{4,3,1,2,0:T(8,128)(2,1)S(1)} fusion(bf16[2,64,4,16,4,64]{5,3,4,1,2,0:T(8,128)(2,1)} %copy.15, f32[2,64,4,16]{3,1,2,0:T(8,128)S(1)} %copy.17, f32[2,64,4,16]{3,1,2,0:T(8,128)S(1)} %copy.14, bf16[4,2,64,4,128,1]{4,3,2,1,0,5:T(4,128)(2,1)S(1)} %bitcast.56), kind=kOutput, calls=%fused_computation.11 | convolution fusion | flops 540016640 | bytes 6881280 | tf_op jit(solution)/shard_map/sqgrnk,nskgd->sqgrd/dot_general | solution.py:110
  77.3 1.9 copy.18
  79.2 2.8 reshape.237
  82.1 1.2 convolution_convert_fusion
  83.3 97.9 %all_to_all.5 = bf16[8,32,8192]{2,1,0:T(8,128)(2,1)S(1)} all-to-all(bf16[8,32,8192]{2,1,0:T(8,128)(2,1)S(1)} %bitcast.49), channel_id=1, replica_groups=mesh['pp'=4,'cp'=4,'tp'=2] {'cp','tp'}, dimensions={0} | all-to-all | bytes 8388608 | tf_op jit(solution)/shard_map/all_to_all | solution.py:40
  181.2 6.4 %copy.19 = bf16[4,2,32,8192]{3,1,2,0:T(2,128)(2,1)} copy(bf16[4,2,32,8192]{3,2,1,0:T(8,128)(2,1)S(1)} %bitcast.50) | data formatting | bytes 8388608 | tf_op jit(solution)/shard_map/reshape | solution.py:41
  187.6 4.8 %copy.31 = bf16[16,8,2,8192]{3,1,2,0:T(8,128)(2,1)S(1)} copy(bf16[16,8,2,8192]{3,2,1,0:T(2,128)(2,1)} %bitcast.51) | data formatting | bytes 8388608
  192.4 1.6 collective-permute-start
  194.0 91.3 %collective-permute-done = bf16[128,16384]{1,0:T(8,128)(2,1)S(1)} collective-permute-done((bf16[128,16384]{1,0:T(8,128)(2,1)S(1)}, bf16[128,16384]{1,0:T(8,128)(2,1)S(1)}, u32[]{:S(2)}, u32[]{:S(2)}) %collective-permute-start) | collective-permute-done | bytes 4194336 | tf_op jit(solution)/shard_map/ppermute | solution.py:13
  285.3 2.0 copy.45
  (26 shorter events, 0.9 us)
Async XLA Ops:
  0.0 0.7 copy-start
  0.0 8.3 %copy-start.2 = (bf16[128,512]{1,0:T(8,128)(2,1)S(1)}, bf16[128,512]{1,0:T(8,128)(2,1)}, u32[]{:S(2)}) copy-start(bf16[128,512]{1,0:T(8,128)(2,1)} %param.7) | copy-start | bytes 393220
  38.0 17.2 %copy-start.3 = (bf16[128,512]{1,0:T(8,128)(2,1)S(1)}, bf16[128,512]{1,0:T(8,128)(2,1)}, u32[]{:S(2)}) copy-start(bf16[128,512]{1,0:T(8,128)(2,1)} %param.8) | copy-start | bytes 393220
  192.4 94.9 %copy-start.1 = (s32[4,128,1]{1,2,0:T(1,128)S(1)}, s32[4,128,1]{1,2,0:T(1,128)}, u32[]{:S(2)}) copy-start(s32[4,128,1]{1,2,0:T(1,128)} %param.11) | copy-start | bytes 6148
  192.4 92.9 %collective-permute-start = (bf16[128,16384]{1,0:T(8,128)(2,1)S(1)}, bf16[128,16384]{1,0:T(8,128)(2,1)S(1)}, u32[]{:S(2)}, u32[]{:S(2)}) collective-permute-start(bf16[128,16384]{1,0:T(8,128)(2,1)S(1)} %bitcast.53), channel_id=1, source_target_pairs={{24,0},{0,8},{8,16},{16,24},{25,1},{1,9},{9,17},{17,25},{26,2},{2,... | collective-permute-start | bytes 12582920 | tf_op jit(solution)/shard_map/ppermute | solution.py:13
where the time goes:
time: 288 us; the launch traced here: 287 us
  blocking collectives  131 us (45%)
  waiting for transfers between devices  91.3 us (32%)
  local copies, waits for them, and re-layouts  42 us (15%)
  matrix products  12.6 us (4%)
  other arithmetic  6.85 us (2%)
    all_to_all x1, blocking collectives, spread_rows(): lax.all_to_all(flat_buffer, ('cp', 'tp'), split_axis=0, concat_axis=0, ti...  97.9 us
    ppermute x1, waiting for transfers between devices, shifted(): return lax.ppermute(block, axis, route)  91.3 us
    all_gather x1, blocking collectives, body(): key_piece = lax.all_gather(keys, 'cp', axis=0, tiled=True)  17.4 us
    convert_element_type x1, local copies, waits for them, and re-layouts, body(): weights.astype(jnp.bfloat16).reshape(stat_shape + (block, 2 * block_len))  17.2 us
    all_gather x1, blocking collectives, body(): value_piece = lax.all_gather(values, 'cp', axis=0, tiled=True)  16.2 us
    unnamed x11, local copies, waits for them, and re-layouts  9.69 us
    reshape x1, local copies, waits for them, and re-layouts, spread_rows(): moved.reshape(cycle_size, split_size, capacity, width)  6.38 us
    reduce_sum x1, other arithmetic, body(): running_total = running_total * carry_factor + jnp.sum(weights, axis=4)  6.22 us
  transfers between devices with their start and end apart: 1, of which 1 were waited for; matrix products, arithmetic and copies ran while one was open for 0% of the time, Pallas kernels for 0%

commit v1 on v0

--- a/solution.py
+++ b/solution.py
@@ -75,8 +75,11 @@
         jnp.zeros(stat_shape + (HD,), jnp.float32),
     )
     state = start_state
-    key_piece = lax.all_gather(keys, "cp", axis=0, tiled=True)
-    value_piece = lax.all_gather(values, "cp", axis=0, tiled=True)
+    key_piece, value_piece = jnp.split(
+        lax.all_gather(jnp.concatenate([keys, values], axis=1), "cp", axis=0, tiled=True),
+        [keys.shape[1]],
+        axis=1,
+    )
     shard_count = key_piece.shape[0] // row_count
     first_shard = jnp.int32(0) // row_count
     for base in range(0, shard_count, 4):

time: 288 us -> 279 us (0.969)
  blocking collectives: 131 us -> 97 us
  waiting for transfers between devices: 91.3 us -> 115 us
  local copies, waits for them, and re-layouts: 42 us -> 27.7 us
  between operations: 1.49 us -> 14.8 us
    all_gather x2 -> x0, blocking collectives: 33.6 us -> none  [the longest x1 17.4 us: body(): key_piece = lax.all_gather(keys, 'cp', axis=0, tiled=True)]
    all_gather x0 -> x1, waiting for transfers between devices: none -> 23.6 us  [body(): lax.all_gather(jnp.concatenate([keys, values], axis=1), 'cp', axis=0, til...]
    convert_element_type x1 -> x0, local copies, waits for them, and re-layouts: 17.2 us -> none  [body(): weights.astype(jnp.bfloat16).reshape(stat_shape + (block, 2 * block_len))]
    unnamed x11 -> x5, local copies, waits for them, and re-layouts: 9.69 us -> 9 us
  transfers between devices with their start and end apart: 1 -> 2, of which waited for: 1 -> 2; matrix products, arithmetic and copies ran while one was open for 0% -> 2% of each run, Pallas kernels for 0% -> 0%
where the time goes in v1:
time: 279 us; the launch traced here: 278 us
  waiting for transfers between devices  115 us (41%)
  blocking collectives  97 us (35%)
  local copies, waits for them, and re-layouts  27.7 us (10%)
  between operations  14.8 us (5%)
  matrix products  13.7 us (5%)
  other arithmetic  8.54 us (3%)
    all_to_all x1, blocking collectives, spread_rows(): lax.all_to_all(flat_buffer, ('cp', 'tp'), split_axis=0, concat_axis=0, ti...  97 us
    ppermute x1, waiting for transfers between devices, shifted(): return lax.ppermute(block, axis, route)  91.4 us
    all_gather x1, waiting for transfers between devices, body(): lax.all_gather(jnp.concatenate([keys, values], axis=1), 'cp', axis=0, til...  23.6 us
    unnamed x5, local copies, waits for them, and re-layouts  9 us
    dot_general x1, matrix products, body(): jnp.einsum('sqgrnk,nskgd->sqgrd', shaped, value_block, preferred_element_...  6.76 us
    reshape x1, local copies, waits for them, and re-layouts, spread_rows(): moved.reshape(cycle_size, split_size, capacity, width)  6.38 us
    reduce_sum x1, other arithmetic, body(): running_total = running_total * carry_factor + jnp.sum(weights, axis=4)  6.21 us
  transfers between devices with their start and end apart: 2, of which 2 were waited for; matrix products, arithmetic and copies ran while one was open for 2% of the time, Pallas kernels for 0%

profile of v1, /device:TPU:0, one launch (start us, length us, event | category | flops | bytes accessed | tf_op | source)
XLA Modules:
  0.0 278.2 jit_solution(16795584549973656999)
XLA Ops:
  6.5 1.7 pad_maximum_fusion
  8.3 0.7 fusion.18
  9.0 1.3 dynamic_slice.18
  11.6 0.6 gather_fusion
  12.2 0.9 dynamic-slice_reduce_fusion
  13.1 2.2 copy.28
  15.3 0.2 fusion.13
  15.9 0.1 broadcast_and_fusion
  16.1 23.6 %all-gather.2.cloned.1.call-done = bf16[512,1024]{1,0:T(8,128)(2,1)} async-done(((bf16[128,1024]{1,0:T(8,128)(2,1)}), bf16[512,1024]{1,0:T(8,128)(2,1)}) %all-gather.2.cloned.1.call-update) | async-done | bytes 1048592 | tf_op jit(solution)/shard_map/all_gather | solution.py:79
  39.6 2.1 fusion.20
  41.7 1.2 reshape.234
  42.8 5.5 %fusion = (f32[2,64,4,16]{1,3,2,0:T(8,128)S(1)}, f32[2,4,4,64,64,16]{4,3,5,2,1,0:T(8,128)S(1)}) fusion(pred[2,64,4,64]{1,3,2,0:T(8,128)(4,1)S(1)} %broadcast_and_fusion, bf16[2,64,4,16,128,1]{4,3,2,1,0,5:T(8,128)(2,1)S(1)} %bitcast.51, bf16[4,2,64,4,128,1]{4,3,2,1,0,5:T(4,128)(2,1)S(1)} %bitcast.53), kind=kOutput, calls=%fused_computation.3 | convolution fusion | flops 543154176 | bytes 11075584 | tf_op jit(solution)/shard_map/sqgrd,nskgd->sqgrnk/dot_general | solution.py:102
  48.4 6.2 %fusion.3 = (f32[2,64,4,16]{1,3,2,0:T(8,128)S(1)}, bf16[2,64,4,16,4,64]{1,5,3,4,2,0:T(8,128)(2,1)}) fusion(f32[2,4,4,64,64,16]{4,3,5,2,1,0:T(8,128)S(1)} %get-tuple-element.14, f32[2,64,4,16]{1,3,2,0:T(8,128)S(1)} %broadcast_maximum_fusion, pred[2,64,4,64]{1,3,2,0:T(8,128)(4,1)S(1)} %broadcast_and_fusion), kind=kLoop, calls=%fused_computation.6 | loop fusion | flops 10477568 | bytes 12681216 | tf_op jit(solution)/shard_map/reduce_sum | solution.py:111
  54.6 0.1 reshape.236
  54.7 6.8 %fusion.8 = bf16[2,64,4,16,128]{4,1,3,2,0:T(8,128)(2,1)S(1)} fusion(bf16[2,64,4,16,4,64]{1,5,3,4,2,0:T(8,128)(2,1)} %get-tuple-element.6, f32[2,64,4,16]{1,3,2,0:T(8,128)S(1)} %get-tuple-element.10, f32[2,64,4,16]{1,3,2,0:T(8,128)S(1)} %get-tuple-element.9, bf16[4,2,64,4,128,1]{4,3,2,1,0,5:T(4,128)(2,1)S(1)} %bitcast.55), kind=kOutput, calls=%fused_computation.13 | convolution fusion | flops 540016640 | bytes 6881280 | tf_op jit(solution)/shard_map/sqgrnk,nskgd->sqgrd/dot_general | solution.py:113
  61.5 2.7 copy.14
  64.2 2.8 %reshape.237 = bf16[128,8192]{1,0:T(8,128)(2,1)S(1)} reshape(bf16[2,64,4,16,128]{4,3,2,1,0:T(8,128)(2,1)} %copy.14) | data formatting | bytes 4194304 | tf_op jit(solution)/shard_map/reshape | solution.py:117
  67.0 1.2 convolution_convert_fusion
  68.3 97.0 %all_to_all.5 = bf16[8,32,8192]{2,1,0:T(8,128)(2,1)S(1)} all-to-all(bf16[8,32,8192]{2,1,0:T(8,128)(2,1)S(1)} %bitcast.48), channel_id=1, replica_groups=mesh['pp'=4,'cp'=4,'tp'=2] {'cp','tp'}, dimensions={0} | all-to-all | bytes 8388608 | tf_op jit(solution)/shard_map/all_to_all | solution.py:40
  165.3 6.4 %copy.15 = bf16[4,2,32,8192]{3,1,2,0:T(2,128)(2,1)} copy(bf16[4,2,32,8192]{3,2,1,0:T(8,128)(2,1)S(1)} %bitcast.49) | data formatting | bytes 8388608 | tf_op jit(solution)/shard_map/reshape | solution.py:41
  171.6 4.8 %copy.29 = bf16[16,8,2,8192]{3,1,2,0:T(8,128)(2,1)S(1)} copy(bf16[16,8,2,8192]{3,2,1,0:T(2,128)(2,1)} %bitcast.50) | data formatting | bytes 8388608
  176.5 1.5 collective-permute-start
  178.0 91.4 %collective-permute-done = bf16[128,16384]{1,0:T(8,128)(2,1)S(1)} collective-permute-done((bf16[128,16384]{1,0:T(8,128)(2,1)S(1)}, bf16[128,16384]{1,0:T(8,128)(2,1)S(1)}, u32[]{:S(2)}, u32[]{:S(2)}) %collective-permute-start) | collective-permute-done | bytes 4194336 | tf_op jit(solution)/shard_map/ppermute | solution.py:13
  269.3 2.0 copy.47
  (20 shorter events, 0.5 us)
Async XLA Ops:
  6.5 8.7 %copy-start = (s32[4,128,1]{1,2,0:T(1,128)S(1)}, s32[4,128,1]{1,2,0:T(1,128)}, u32[]{:S(2)}) copy-start(s32[4,128,1]{1,2,0:T(1,128)} %param.11) | copy-start | bytes 6148
  6.5 33.1 %all-gather.2.cloned.1.call-start = ((), (), s32[]{:S(2)}) async-start(), calls=%async_computation.1 | async-start | bytes 1310720 | tf_op jit(solution)/shard_map/all_gather | solution.py:79
  176.5 92.9 %collective-permute-start = (bf16[128,16384]{1,0:T(8,128)(2,1)S(1)}, bf16[128,16384]{1,0:T(8,128)(2,1)S(1)}, u32[]{:S(2)}, u32[]{:S(2)}) collective-permute-start(bf16[128,16384]{1,0:T(8,128)(2,1)S(1)} %bitcast.52), channel_id=1, source_target_pairs={{24,0},{0,8},{8,16},{16,24},{25,1},{1,9},{9,17},{17,25},{26,2},{2,... | collective-permute-start | bytes 12582920 | tf_op jit(solution)/shard_map/ppermute | solution.py:13
Sparse Core Ops, SparseCore 0:
  8.9 30.6 all-gather.1
